TPU v7x, 512 devices: a whole 4x8x8 slice. The times are simulated.
512 devices in a mesh: dp: 32 (over x, z), tp: 16 (over y, core).
Axes of the slice: x: 4, y: 8, z: 8, core: 2. Of those that a mesh axis runs over, the one named last changes fastest.
Arguments:
- queries: bfloat16 [1024, 128, 576], P(('dp', 'tp')), may hold values from -40 to 40
- latent_cache: bfloat16 [1024, 256, 576], P(('dp', 'tp')), may hold values from -5 to 5
- lengths: int32 [1024], P(('dp', 'tp')), may hold values from 1 to 256, 65536 in all
- value_weight: bfloat16 [128, 512, 128], P('tp'), may hold values from -0.25 to 0.25
- output_weight: bfloat16 [16384, 7168], P('tp', 'dp'), may hold values from -0.046875 to 0.046875
Outputs:
- attended: bfloat16 [1024, 7168], P(('dp', 'tp'))
All inputs are finite; a program needn't handle non-finite values. No bound on the sum of `lengths` on one device may be relied on, other than what follows from the above.
Results may differ from a plain program's by a relative error of at most 0.0065.
Values may be sent and summed in bfloat16 or wider, within the bound.
No kernel may reach another device: no remote copies, remote signals or barrier semaphores. Data moves between devices by JAX's collectives and lax.ppermute only.
A program may use at most 64 MiB of HBM per device.

v0:
```python
import jax
import jax.numpy as jnp
from jax import lax
from jax.sharding import PartitionSpec as P

score_scale = 192.0 ** (-0.5)


def local(queries, latent_cache, lengths, value_weight, output_weight):
    requests = queries.shape[0]
    groups = lax.axis_size("tp")
    columns = lax.axis_size("dp")
    latent_width = value_weight.shape[1]
    scores = (
        jnp.einsum("rhe,rje->rhj", queries, latent_cache, preferred_element_type=jnp.float32)
        * score_scale
    )
    alive_mask = lax.broadcasted_iota(jnp.int32, scores.shape, 2) < lengths[:, None, None]
    scores = jnp.where(alive_mask, scores, -1e30)
    row_max = jnp.max(scores, axis=2, keepdims=True)
    powers = jnp.exp(scores - row_max)
    weights = (powers / jnp.sum(powers, axis=2, keepdims=True)).astype(jnp.bfloat16)
    mixture = jnp.einsum("rhj,rje->rhe", weights, latent_cache, preferred_element_type=jnp.float32)
    latent = mixture[:, :, :latent_width].astype(jnp.bfloat16)
    swapped = lax.all_to_all(latent, "tp", split_axis=1, concat_axis=0, tiled=True)
    values = jnp.einsum("qhd,hde->qhe", swapped, value_weight, preferred_element_type=jnp.float32)
    values = values.astype(jnp.bfloat16).reshape(groups, requests, -1)
    everyone = lax.all_gather(values, "dp", axis=1, tiled=True)
    all_values = everyone.reshape(groups * columns * requests, -1)
    summed = lax.psum_scatter(
        jnp.dot(all_values, output_weight, preferred_element_type=jnp.float32),
        "tp",
        scatter_dimension=0,
        tiled=True,
    )
    rounded = summed.astype(jnp.bfloat16)
    return lax.all_to_all(rounded, "dp", split_axis=0, concat_axis=1, tiled=True)


def solution(mesh):
    return jax.shard_map(
        local,
        mesh=mesh,
        in_specs=(
            P(("dp", "tp"), None, None),
            P(("dp", "tp"), None, None),
            P(("dp", "tp")),
            P("tp", None, None),
            P("tp", "dp"),
        ),
        out_specs=P(("dp", "tp"), None),
        check_vma=False,
    )
```

profile of v0, /device:TPU:2, one launch (start us, length us, event | category | flops | bytes accessed | tf_op | source)
XLA Modules:
  0.0 203.4 jit_solution(8184634764328297941)
XLA Ops:
  6.5 0.0 copy-start
  6.5 0.0 all-gather.2.cloned.1.call-start
  6.5 1.5 fusion.3
  8.1 0.2 fusion.8
  8.3 1.6 fusion.5
  9.9 0.3 copy.16
  10.2 18.2 %all_to_all.37 = bf16[2,128,512]{2,0,1:T(2,128)(2,1)S(1)} all-to-all(bf16[2,128,512]{2,0,1:T(2,128)(2,1)S(1)} %copy.16), channel_id=1, replica_groups=mesh['dp'=32,'tp'=16] {'tp'}, dimensions={1} | all-to-all | bytes 524288 | tf_op jit(solution)/shard_map/all_to_all | solution.py:25
  28.4 0.2 copy.23
  28.6 0.1 all_to_all.30
  28.7 0.0 copy-done
  28.7 0.3 fusion.4
  29.0 0.6 copy.19
  29.7 0.0 all-gather.2.cloned.1.call-update
  29.7 0.0 copy-start.1
  29.7 0.0 reduce-scatter.2.cloned.1.call-start
  29.7 83.9 %all-gather.2.cloned.1.call-done = bf16[16,64,1024]{2,0,1:T(8,128)(2,1)} async-done(((bf16[16,2,1024]{2,0,1:T(8,128)(2,1)}), bf16[16,64,1024]{2,0,1:T(8,128)(2,1)}) %all-gather.2.cloned.1.call-update) | async-done | bytes 2097168 | tf_op jit(solution)/shard_map/all_gather | solution.py:28
  113.6 2.7 %copy.20 = bf16[16,64,1024]{2,1,0:T(8,128)(2,1)S(1)} copy(bf16[16,64,1024]{2,0,1:T(8,128)(2,1)} %all-gather.2.cloned.1.call-done) | data formatting | bytes 4194304 | tf_op jit(solution)/shard_map/all_gather | solution.py:28
  116.4 0.0 copy-done.1
  116.4 1.7 fusion.9
  118.1 0.0 reduce-scatter.2.cloned.1.call-update
  118.2 57.8 %reduce-scatter.2.cloned.1.call-done = f32[64,224]{1,0:T(8,128)} async-done(((f32[1024,224]{1,0:T(8,128)}), f32[64,224]{1,0:T(8,128)}) %reduce-scatter.2.cloned.1.call-update) | async-done | bytes 57360 | tf_op jit(solution)/shard_map/reduce_scatter | solution.py:30
  175.9 0.8 convert_element_type.16
  176.8 19.0 %all_to_all.38 = bf16[32,2,224]{2,1,0:T(2,128)(2,1)S(1)} all-to-all(bf16[32,2,224]{2,1,0:T(2,128)(2,1)S(1)} %all_to_all.31), channel_id=1, replica_groups=mesh['dp'=32,'tp'=16] {'dp'}, dimensions={0} | all-to-all | bytes 57344 | tf_op jit(solution)/shard_map/all_to_all | solution.py:37
  195.8 0.7 all_to_all.34
  (5 shorter events, 0.1 us)
Async XLA Ops:
  6.5 22.1 %copy-start = (bf16[8,512,128]{2,1,0:T(8,128)(2,1)S(1)}, bf16[8,512,128]{2,1,0:T(8,128)(2,1)}, u32[]{:S(2)}) copy-start(bf16[8,512,128]{2,1,0:T(8,128)(2,1)} %param.8) | copy-start | bytes 3145732
  6.5 107.1 %all-gather.2.cloned.1.call-start = ((), (), s32[]{:S(2)}) async-start(), calls=%async_computation.3 | async-start | bytes 2162688 | tf_op jit(solution)/shard_map/all_gather | solution.py:28
  29.7 86.7 %copy-start.1 = (bf16[1024,224]{0,1:T(8,128)(2,1)S(1)}, bf16[1024,224]{0,1:T(8,128)(2,1)}, u32[]{:S(2)}) copy-start(bf16[1024,224]{0,1:T(8,128)(2,1)} %param.9) | copy-start | bytes 1376260
  29.7 146.2 %reduce-scatter.2.cloned.1.call-start = ((), (), s32[]{:S(2)}) async-start(), calls=%async_computation.4 | async-start | bytes 1114112 | tf_op jit(solution)/shard_map/reduce_scatter | solution.py:30
Sparse Core Ops, SparseCore 0:
  29.8 83.7 all-gather.1
  118.3 57.6 reduce-scatter.1
where the time goes:
time: 204 us; the launch traced here: 203 us
  waiting for transfers between devices  142 us (70%)
  blocking collectives  37.2 us (18%)
  between operations  13.5 us (7%)
  matrix products  5.14 us (3%)
  local copies, waits for them, and re-layouts  4.78 us (2%)
    all_gather x1, waiting for transfers between devices, local(): everyone = lax.all_gather(values, 'dp', axis=1, tiled=True)  83.9 us
    reduce_scatter x1, waiting for transfers between devices, local(): lax.psum_scatter(jnp.dot(all_values, output_weight, preferred_element_typ...  57.8 us
    all_to_all x1, blocking collectives, local(): lax.all_to_all(rounded, 'dp', split_axis=0, concat_axis=1, tiled=True)  19 us
    all_to_all x1, blocking collectives, local(): lax.all_to_all(latent, 'tp', split_axis=1, concat_axis=0, tiled=True)  18.2 us
  transfers between devices with their start and end apart: 2, of which 2 were waited for; matrix products, arithmetic and copies ran while one was open for 0% of the time, Pallas kernels for 0%

commit v1 on v0

--- a/solution.py
+++ b/solution.py
@@ -2,6 +2,7 @@
 import jax.numpy as jnp
 from jax import lax
 from jax.sharding import PartitionSpec as P
+from jax.lax import all_to_all, axis_size
 
 score_scale = 192.0 ** (-0.5)
 
@@ -25,7 +26,9 @@
     swapped = lax.all_to_all(latent, "tp", split_axis=1, concat_axis=0, tiled=True)
     values = jnp.einsum("qhd,hde->qhe", swapped, value_weight, preferred_element_type=jnp.float32)
     values = values.astype(jnp.bfloat16).reshape(groups, requests, -1)
-    everyone = lax.all_gather(values, "dp", axis=1, tiled=True)
+    everyone = jnp.concatenate(
+        all_to_all(jnp.stack(axis_size("dp") * [values], axis=0), "dp", 0, 0), axis=1
+    )
     all_values = everyone.reshape(groups * columns * requests, -1)
     summed = lax.psum_scatter(
         jnp.dot(all_values, output_weight, preferred_element_type=jnp.float32),

time: 204 us -> 185 us (0.907)
  waiting for transfers between devices: 142 us -> 54.4 us
  blocking collectives: 37.2 us -> 99.7 us
  local copies, waits for them, and re-layouts: 4.78 us -> 9.4 us
    all_gather x1 -> x0, waiting for transfers between devices: 83.9 us -> none  [local(): everyone = lax.all_gather(values, 'dp', axis=1, tiled=True)]
    all_to_all x0 -> x1, blocking collectives: none -> 62.7 us  [local(): all_to_all(jnp.stack(axis_size('dp') * [values], axis=0), 'dp', 0, 0)]
    another operation x0 -> x3, local copies, waits for them, and re-layouts: none -> 4.65 us  [the longest x1 2.75 us: local(): all_values = everyone.reshape(groups * columns * requests, -1)]
    reduce_scatter x1, waiting for transfers between devices: 57.8 us -> 54.3 us  [local(): lax.psum_scatter(jnp.dot(all_values, output_weight, preferred_element_typ...]
    all_gather x1 -> x0, local copies, waits for them, and re-layouts: 2.74 us -> none  [local(): everyone = lax.all_gather(values, 'dp', axis=1, tiled=True)]
    reshape x2 -> x1, local copies, waits for them, and re-layouts: 0.66 us -> 3.37 us  [local(): jnp.concatenate(all_to_all(jnp.stack(axis_size('dp') * [values], axis=0),...]
  transfers between devices with their start and end apart: 2 -> 1, of which waited for: 2 -> 1; matrix products, arithmetic and copies ran while one was open for 0% -> 0% of each run, Pallas kernels for 0% -> 0%
where the time goes in v1:
time: 185 us; the launch traced here: 184 us
  blocking collectives  99.7 us (54%)
  waiting for transfers between devices  54.4 us (29%)
  between operations  13.5 us (7%)
  local copies, waits for them, and re-layouts  9.4 us (5%)
  matrix products  6.16 us (3%)
    all_to_all x1, blocking collectives, local(): all_to_all(jnp.stack(axis_size('dp') * [values], axis=0), 'dp', 0, 0)  62.7 us
    reduce_scatter x1, waiting for transfers between devices, local(): lax.psum_scatter(jnp.dot(all_values, output_weight, preferred_element_typ...  54.3 us
    all_to_all x1, blocking collectives, local(): lax.all_to_all(rounded, 'dp', split_axis=0, concat_axis=1, tiled=True)  18.8 us
    all_to_all x1, blocking collectives, local(): lax.all_to_all(latent, 'tp', split_axis=1, concat_axis=0, tiled=True)  18.2 us
  transfers between devices with their start and end apart: 1, of which 1 were waited for; matrix products, arithmetic and copies ran while one was open for 0% of the time, Pallas kernels for 0%

profile of v1, /device:TPU:2, one launch (start us, length us, event | category | flops | bytes accessed | tf_op | source)
XLA Modules:
  0.0 184.1 jit_solution(16310146627851482384)
XLA Ops:
  6.5 0.0 copy-start
  6.5 0.0 reduce-scatter.2.cloned.1.call-start
  6.5 1.5 fusion.3
  8.1 0.2 fusion.8
  8.3 1.6 fusion.5
  9.9 0.3 copy.11
  10.2 18.2 %all_to_all.42 = bf16[2,128,512]{2,0,1:T(2,128)(2,1)S(1)} all-to-all(bf16[2,128,512]{2,0,1:T(2,128)(2,1)S(1)} %copy.11), channel_id=1, replica_groups=mesh['dp'=32,'tp'=16] {'tp'}, dimensions={1} | all-to-all | bytes 524288 | tf_op jit(solution)/shard_map/all_to_all | solution.py:26
  28.4 0.2 copy.17
  28.6 0.1 all_to_all.33
  28.7 0.0 copy-done
  28.7 0.3 fusion.4
  29.0 1.9 %stack.3 = bf16[32,16,2,1024]{3,2,1,0:T(2,128)(2,1)S(1)} broadcast(bf16[16,2,1024]{2,1,0:T(2,128)(2,1)S(1)} %stack_reshape.2), dimensions={1,2,3} | broadcast | bytes 2162688 | tf_op jit(solution)/shard_map/stack | solution.py:30
  30.9 62.7 %all_to_all.43 = bf16[32,16,2,1024]{3,2,1,0:T(2,128)(2,1)S(1)} all-to-all(bf16[32,16,2,1024]{3,2,1,0:T(2,128)(2,1)S(1)} %stack.3), channel_id=1, replica_groups=mesh['dp'=32,'tp'=16] {'dp'}, dimensions={0} | all-to-all | bytes 4194304 | tf_op jit(solution)/shard_map/all_to_all | solution.py:30
  93.6 3.4 %copy.14 = bf16[16,32,2,1024]{3,2,1,0:T(2,128)(2,1)} copy(bf16[16,32,2,1024]{3,2,0,1:T(2,128)(2,1)S(1)} %bitcast.19) | data formatting | bytes 4194304 | tf_op jit(solution)/shard_map/reshape | solution.py:29
  97.0 2.7 %reshape_reshape.3 = bf16[1024,1024]{1,0:T(8,128)(2,1)S(1)} reshape(bf16[16,32,2,1024]{3,2,1,0:T(2,128)(2,1)} %copy.14) | data formatting | bytes 4194304 | tf_op jit(solution)/shard_map/reshape;reshape | solution.py:32
  99.7 2.7 %fusion.9 = f32[1024,224]{1,0:T(8,128)} fusion(bf16[1024,1024]{1,0:T(8,128)(2,1)S(1)} %reshape_reshape.3, bf16[1024,224]{0,1:T(8,128)(2,1)} %param.9), kind=kOutput, calls=%fused_computation.15 | convolution fusion | flops 469762048 | bytes 3473408 | tf_op jit(solution)/shard_map/dot_general | solution.py:34
  102.5 0.0 reduce-scatter.2.cloned.1.call-update
  102.5 54.3 %reduce-scatter.2.cloned.1.call-done = f32[64,224]{1,0:T(8,128)} async-done(((f32[1024,224]{1,0:T(8,128)}), f32[64,224]{1,0:T(8,128)}) %reduce-scatter.2.cloned.1.call-update) | async-done | bytes 57360 | tf_op jit(solution)/shard_map/reduce_scatter | solution.py:33
  156.9 0.8 convert_element_type.16
  157.7 18.8 %all_to_all.44 = bf16[32,2,224]{2,1,0:T(2,128)(2,1)S(1)} all-to-all(bf16[32,2,224]{2,1,0:T(2,128)(2,1)S(1)} %all_to_all.35), channel_id=1, replica_groups=mesh['dp'=32,'tp'=16] {'dp'}, dimensions={0} | all-to-all | bytes 57344 | tf_op jit(solution)/shard_map/all_to_all | solution.py:40
  176.5 0.7 all_to_all.38
  (5 shorter events, 0.1 us)
Async XLA Ops:
  6.5 22.1 %copy-start = (bf16[8,512,128]{2,1,0:T(8,128)(2,1)S(1)}, bf16[8,512,128]{2,1,0:T(8,128)(2,1)}, u32[]{:S(2)}) copy-start(bf16[8,512,128]{2,1,0:T(8,128)(2,1)} %param.8) | copy-start | bytes 3145732
  6.5 150.3 %reduce-scatter.2.cloned.1.call-start = ((), (), s32[]{:S(2)}) async-start(), calls=%async_computation.4 | async-start | bytes 1114112 | tf_op jit(solution)/shard_map/reduce_scatter | solution.py:33
Sparse Core Ops, SparseCore 0:
  102.6 54.1 reduce-scatter.1
